TPU v7x, 32 devices: a whole 2x2x4 slice. The times are simulated.
32 devices in a mesh: scan: 8 (over y, x, core), tile: 4 (over z).
Axes of the slice: x: 2, y: 2, z: 4, core: 2. Of those that a mesh axis runs over, the one named last changes fastest.
Arguments:
- object_field: float32 [2, 2048, 1024], P(None, 'scan', 'tile'), may hold values from -4.2 to 4.2
- probe_modes: float32 [8, 2, 256, 256], P('tile'), may hold values from -2.1 to 2.1
- amplitudes: bfloat16 [64, 256, 256], P('scan'), may hold values from 0.25 to 3
- positions: int32 [64, 2], P('scan'), may hold values from 0 to 1792, as said below
- counts: int32 [8], P('scan'), may hold values from 1 to 8, as said below
Outputs:
- new_object: float32 [2, 2048, 1024], P(None, 'scan', 'tile')
- probe_step: float32 [8, 2, 256, 256], P('tile')
Inputs may be any that keep to these rules, and one draw needn't show every extreme that they name: `positions`: slot j's row offset lies in rows (j // 8) * 256 to (j // 8) * 256 + 255; every window lies inside the object: row offsets at most 1792, column offsets at most 768. `counts`: some scan index holds 8 live slots and some holds one.
All inputs are finite; a program needn't handle non-finite values.
Results may differ from a plain program's by a relative error of at most 0.003.
Values may be sent and summed in bfloat16 or wider, within the bound.
No kernel may reach another device: no remote copies, remote signals or barrier semaphores. Data moves between devices by JAX's collectives and lax.ppermute only.
A program may use at most 128 MiB of HBM per device.

v0:
```python
import math
import jax
import jax.numpy as jnp
from jax import lax
from jax.sharding import PartitionSpec as P

damping = 1.0
amp_floor = 0.5


def passed_along(value, axis, steps):
    count = lax.axis_size(axis)
    leading, last = (max(0, -steps), min(count, count - steps))
    return lax.ppermute(value, axis, [(source, source + steps) for source in range(leading, last)])


def dft_tables(win_width):
    index_row = jnp.arange(win_width, dtype=jnp.int32)
    products = index_row[:, None] * index_row[None, :] % win_width
    phase_angle = products.astype(jnp.float32) * (2.0 * math.pi / win_width)
    norm_scale = 1.0 / math.sqrt(win_width)
    real_part = (jnp.cos(phase_angle) * norm_scale).astype(jnp.bfloat16)
    imag_part = (-jnp.sin(phase_angle) * norm_scale).astype(jnp.bfloat16)
    return (real_part, imag_part)


def transform(rowform, right_table, left_table, win_width):
    half_done = jnp.einsum(
        "mak,kl->mal", rowform, right_table, preferred_element_type=jnp.float32
    ).astype(jnp.bfloat16)
    full_block = jnp.einsum(
        "ca,mak->mck", left_table, half_done, preferred_element_type=jnp.float32
    )
    real_out = full_block[..., :win_width, :win_width] - full_block[..., win_width:, win_width:]
    imag_out = full_block[..., :win_width, win_width:] + full_block[..., win_width:, :win_width]
    return (real_out, imag_out)


def shards(object_field, probe_modes, amplitudes, positions, counts):
    slot_count = amplitudes.shape[0]
    win_width = amplitudes.shape[1]
    band_rows = object_field.shape[1]
    first_row = lax.axis_index("scan") * band_rows
    object_low = object_field.astype(jnp.bfloat16)
    lower_rows = passed_along(object_low, "scan", -1)
    extended = jnp.concatenate([object_low, lower_rows], axis=1)
    band_all = lax.all_gather(extended, "tile", axis=2, tiled=True)
    row_offsets = positions[:, 0] - first_row
    col_offsets = positions[:, 1]
    zero_index = jnp.zeros((), jnp.int32)

    def cut_window(row_at, col_at):
        return lax.dynamic_slice(band_all, (zero_index, row_at, col_at), (2, win_width, win_width))

    windows = jax.vmap(cut_window)(row_offsets, col_offsets)
    slot_ids = jnp.arange(slot_count, dtype=jnp.int32)
    live_mask = (slot_ids < counts[0]).astype(jnp.float32)
    real_part, imag_part = dft_tables(win_width)
    right_fwd = jnp.block([[real_part, imag_part], [-imag_part, real_part]])
    left_fwd = jnp.concatenate([real_part, imag_part], axis=0)
    right_inv = jnp.block([[real_part, -imag_part], [imag_part, real_part]])
    left_inv = jnp.concatenate([real_part, -imag_part], axis=0)
    probe_re = probe_modes[:, 0]
    probe_im = probe_modes[:, 1]
    probe_power = jnp.sum(probe_re * probe_re + probe_im * probe_im, axis=0)

    def forward_one(window):
        window_re = window[0].astype(jnp.float32)
        window_im = window[1].astype(jnp.float32)
        exit_wave = jnp.concatenate(
            [
                probe_re * window_re - probe_im * window_im,
                probe_re * window_im + probe_im * window_re,
            ],
            axis=-1,
        ).astype(jnp.bfloat16)
        far_re, far_im = transform(exit_wave, right_fwd, left_fwd, win_width)
        return (far_re, far_im, jnp.sum(far_re * far_re + far_im * far_im, axis=0))

    far_re, far_im, local_power = lax.map(forward_one, windows)
    intensity = lax.psum(local_power, "tile")
    factor = live_mask[:, None, None] * (
        amplitudes.astype(jnp.float32) / jnp.maximum(jnp.sqrt(intensity), amp_floor) - 1.0
    )
    channels = 3

    def accumulate(running, inputs):
        buffer, grad_sum, weight_sum = running
        slot_re, slot_im, slot_factor, window, live, row_at, col_at = inputs
        change = jnp.concatenate([slot_factor * slot_re, slot_factor * slot_im], axis=-1).astype(
            jnp.bfloat16
        )
        near_re, near_im = transform(change, right_inv, left_inv, win_width)
        window_re = window[0].astype(jnp.float32)
        window_im = window[1].astype(jnp.float32)
        numer_parts = [
            jnp.sum(probe_re * near_re + probe_im * near_im, axis=0),
            jnp.sum(probe_re * near_im - probe_im * near_re, axis=0),
        ]
        numer_parts.append(live * probe_power)
        numer = jnp.stack(numer_parts)
        grads = jnp.stack(
            [window_re * near_re + window_im * near_im, window_re * near_im - window_im * near_re],
            axis=1,
        )
        weight = window_re * window_re + window_im * window_im
        region = lax.dynamic_slice(
            buffer, (zero_index, row_at, col_at), (channels, win_width, win_width)
        )
        buffer = lax.dynamic_update_slice(buffer, region + numer, (zero_index, row_at, col_at))
        return ((buffer, grad_sum + grads, weight_sum + live * weight), None)

    init = (
        jnp.zeros((channels, band_rows + win_width, band_all.shape[2]), jnp.float32),
        jnp.zeros(probe_modes.shape, jnp.float32),
        jnp.zeros((win_width, win_width), jnp.float32),
    )
    (buffer, grad_sum, weight_sum), _ = lax.scan(
        accumulate, init, (far_re, far_im, factor, windows, live_mask, row_offsets, col_offsets)
    )
    rim_rows = passed_along(buffer[:, band_rows:, :].astype(jnp.bfloat16), "scan", 1).astype(
        jnp.float32
    )
    own_rows = buffer[:, :band_rows, :].at[:, :win_width, :].add(rim_rows)
    totals = lax.psum_scatter(own_rows, "tile", scatter_dimension=2, tiled=True)
    illumination = totals[2]
    new_object = object_field + totals[0:2] / (illumination + damping)[None]
    grad_total, weight_total = lax.psum((grad_sum, weight_sum), "scan")
    probe_step = grad_total / (weight_total + damping)[None, None]
    return (new_object, probe_step)


def solution(mesh):
    placed = (
        P(None, "scan", "tile"),
        P("tile", None, None, None),
        P("scan", None, None),
        P("scan", None),
        P("scan"),
    )
    return jax.shard_map(
        shards,
        mesh=mesh,
        in_specs=placed,
        out_specs=(P(None, "scan", "tile"), P("tile", None, None, None)),
        check_vma=False,
    )
```

profile of v0, /device:TPU:0, one launch (start us, length us, event | category | flops | bytes accessed | tf_op | source)
XLA Modules:
  0.0 640.8 jit_solution(17734044107008832897)
XLA Ops:
  18.0 47.6 %all-gather.2.cloned.1.call-done = bf16[2,512,1024]{2,1,0:T(8,128)(2,1)} async-done(((bf16[2,512,256]{2,1,0:T(8,128)(2,1)}), bf16[2,512,1024]{2,1,0:T(8,128)(2,1)}) %all-gather.2.cloned.1.call-update) | async-done | bytes 2097168 | tf_op jit(solution)/shard_map/all_gather | solution.py:47
  65.5 30.1 %while.33 = (s32[]{:T(128)}, bf16[2,512,1024]{2,1,0:T(8,128)(2,1)}, s32[8,3]{0,1:T(4,128)S(1)}, bf16[8,2,256,256]{3,2,1,0:T(8,128)(2,1)}, s32[]{:T(128)}) while((s32[]{:T(128)}, bf16[2,512,1024]{2,1,0:T(8,128)(2,1)}, s32[8,3]{0,1:T(4,128)S(1)}, bf16[8,2,256,256]{3,2,1,0:T(8,128)(2,1)}, s32[]{:T(128)}) %tuple.102), condition=%wide.while_cond.1, body=%wide.while_body.1.sunk | while | flops 2 | bytes 525429 | solution.py:53
  66.1 3.2 bitcast_dynamic-update-slice_fusion.6
  69.9 3.1 bitcast_dynamic-update-slice_fusion.6
  73.6 3.2 bitcast_dynamic-update-slice_fusion.6
  77.4 3.2 bitcast_dynamic-update-slice_fusion.6
  81.2 3.2 bitcast_dynamic-update-slice_fusion.6
  85.0 3.2 bitcast_dynamic-update-slice_fusion.6
  88.7 3.2 bitcast_dynamic-update-slice_fusion.6
  92.5 3.2 bitcast_dynamic-update-slice_fusion.6
  95.7 42.0 %while.32 = (s32[]{:T(128)}, f32[8,2,256,256]{2,3,1,0:T(8,128)}, f32[8,2,256,256]{2,3,1,0:T(8,128)}, f32[8,256,256]{2,1,0:T(8,128)}, bf16[8,2,256,256]{3,2,1,0:T...) while((s32[]{:T(128)}, f32[8,2,256,256]{2,3,1,0:T(8,128)}, ...), condition=%wide.region_2.3_spmd, body=%wide.region_0.2_spmd.sunk | while | flops 540344320 | bytes 12845209 | solution.py:80
  142.9 79.3 %all-reduce.4.cloned.1.call-done = f32[8,256,256]{2,1,0:T(8,128)} async-done(((f32[8,256,256]{2,1,0:T(8,128)}), f32[8,256,256]{2,1,0:T(8,128)}) %all-reduce.4.cloned.1.call-update) | async-done | bytes 2097168 | tf_op jit(solution)/shard_map/psum | solution.py:81
  222.2 3.8 add_multiply_fusion
  226.0 3.5 broadcast_in_dim.23.clone
  229.4 267.6 %while.34 = (s32[]{:T(128)}, f32[3,512,1024]{2,1,0:T(8,128)}, f32[2,2,256,256]{2,3,0,1:T(8,128)}, f32[256,256]{0,1:T(8,128)}, s32[8]{0:T(128)S(1)}, /*index=5*/s...) while((s32[]{:T(128)}, f32[3,512,1024]{2,1,0:T(8,128)}, ...), condition=%wide.region_8.9_spmd.clone, body=%wide.region_5.8_spmd.clone.sunk | while | flops 542769152 | bytes 35914140 | solution.py:118
  252.2 8.3 %dynamic_update_slice.23 = f32[3,512,1024]{2,1,0:T(8,128)} dynamic-update-slice(f32[3,512,1024]{2,1,0:T(8,128)} %get-tuple-element.660, f32[3,256,256]{2,1,0:T(8,128)S(1)} %copy.58, s32[]{:T(128)} %constant.100.clone.1..sunk.1, s32[]{:T(128)S(6)} %select_n.65, s32[]{:T(128)S(6)} %select_n.66) | dynamic-update-slice | bytes 1572868 | tf_op jit(solution)/shard_map/while/body/eval_jaxpr/dynamic_update_slice | solution.py:110
  267.4 2.4 select_add_fusion.2
  285.3 7.4 %dynamic_update_slice.23 = f32[3,512,1024]{2,1,0:T(8,128)} dynamic-update-slice(f32[3,512,1024]{2,1,0:T(8,128)} %get-tuple-element.660, f32[3,256,256]{2,1,0:T(8,128)S(1)} %copy.58, s32[]{:T(128)} %constant.100.clone.1..sunk.1, s32[]{:T(128)S(6)} %select_n.65, s32[]{:T(128)S(6)} %select_n.66) | dynamic-update-slice | bytes 1572868 | tf_op jit(solution)/shard_map/while/body/eval_jaxpr/dynamic_update_slice | solution.py:110
  299.6 2.4 select_add_fusion.2
  317.7 9.4 %dynamic_update_slice.23 = f32[3,512,1024]{2,1,0:T(8,128)} dynamic-update-slice(f32[3,512,1024]{2,1,0:T(8,128)} %get-tuple-element.660, f32[3,256,256]{2,1,0:T(8,128)S(1)} %copy.58, s32[]{:T(128)} %constant.100.clone.1..sunk.1, s32[]{:T(128)S(6)} %select_n.65, s32[]{:T(128)S(6)} %select_n.66) | dynamic-update-slice | bytes 1572868 | tf_op jit(solution)/shard_map/while/body/eval_jaxpr/dynamic_update_slice | solution.py:110
  333.9 2.4 select_add_fusion.2
  352.0 8.7 %dynamic_update_slice.23 = f32[3,512,1024]{2,1,0:T(8,128)} dynamic-update-slice(f32[3,512,1024]{2,1,0:T(8,128)} %get-tuple-element.660, f32[3,256,256]{2,1,0:T(8,128)S(1)} %copy.58, s32[]{:T(128)} %constant.100.clone.1..sunk.1, s32[]{:T(128)S(6)} %select_n.65, s32[]{:T(128)S(6)} %select_n.66) | dynamic-update-slice | bytes 1572868 | tf_op jit(solution)/shard_map/while/body/eval_jaxpr/dynamic_update_slice | solution.py:110
  385.6 8.8 %dynamic_update_slice.23 = f32[3,512,1024]{2,1,0:T(8,128)} dynamic-update-slice(f32[3,512,1024]{2,1,0:T(8,128)} %get-tuple-element.660, f32[3,256,256]{2,1,0:T(8,128)S(1)} %copy.58, s32[]{:T(128)} %constant.100.clone.1..sunk.1, s32[]{:T(128)S(6)} %select_n.65, s32[]{:T(128)S(6)} %select_n.66) | dynamic-update-slice | bytes 1572868 | tf_op jit(solution)/shard_map/while/body/eval_jaxpr/dynamic_update_slice | solution.py:110
  401.4 2.4 select_add_fusion.2
  419.4 9.2 %dynamic_update_slice.23 = f32[3,512,1024]{2,1,0:T(8,128)} dynamic-update-slice(f32[3,512,1024]{2,1,0:T(8,128)} %get-tuple-element.660, f32[3,256,256]{2,1,0:T(8,128)S(1)} %copy.58, s32[]{:T(128)} %constant.100.clone.1..sunk.1, s32[]{:T(128)S(6)} %select_n.65, s32[]{:T(128)S(6)} %select_n.66) | dynamic-update-slice | bytes 1572868 | tf_op jit(solution)/shard_map/while/body/eval_jaxpr/dynamic_update_slice | solution.py:110
  453.5 9.1 %dynamic_update_slice.23 = f32[3,512,1024]{2,1,0:T(8,128)} dynamic-update-slice(f32[3,512,1024]{2,1,0:T(8,128)} %get-tuple-element.660, f32[3,256,256]{2,1,0:T(8,128)S(1)} %copy.58, s32[]{:T(128)} %constant.100.clone.1..sunk.1, s32[]{:T(128)S(6)} %select_n.65, s32[]{:T(128)S(6)} %select_n.66) | dynamic-update-slice | bytes 1572868 | tf_op jit(solution)/shard_map/while/body/eval_jaxpr/dynamic_update_slice | solution.py:110
  469.6 2.4 select_add_fusion.2
  487.6 9.4 %dynamic_update_slice.23 = f32[3,512,1024]{2,1,0:T(8,128)} dynamic-update-slice(f32[3,512,1024]{2,1,0:T(8,128)} %get-tuple-element.660, f32[3,256,256]{2,1,0:T(8,128)S(1)} %copy.58, s32[]{:T(128)} %constant.100.clone.1..sunk.1, s32[]{:T(128)S(6)} %select_n.65, s32[]{:T(128)S(6)} %select_n.66) | dynamic-update-slice | bytes 1572868 | tf_op jit(solution)/shard_map/while/body/eval_jaxpr/dynamic_update_slice | solution.py:110
  499.2 4.5 collective-permute-start.1
  505.8 4.9 convert_add_fusion
  510.7 58.9 %all-reduce.6.cloned.1.call-done = (f32[2,2,256,256]{3,2,1,0:T(8,128)}, f32[256,256]{0,1:T(8,128)}) async-done(((f32[2,2,256,256]{3,2,1,0:T(8,128)}, f32[256,256]{0,1:T(8,128)}), (f32[2,2,256,256]{3,2,1,0:T(8,128)}, f32[256,256]{0,1:T(8,128)})) %all-reduce.6.cloned.1.call-update) | async-done | bytes 1310736 | tf_op jit(solution)/shard_map/psum | solution.py:128
  573.0 58.3 %reduce-scatter.2.cloned.1.call-done = f32[3,256,256]{2,1,0:T(8,128)} async-done(((f32[3,256,1024]{2,1,0:T(8,128)}), f32[3,256,256]{2,1,0:T(8,128)}) %reduce-scatter.2.cloned.1.call-update) | async-done | bytes 786448 | tf_op jit(solution)/shard_map/reduce_scatter | solution.py:125
  (327 shorter events, 226.3 us)
Async XLA Ops:
  7.2 5.7 copy-start.8
  7.2 58.4 %all-gather.2.cloned.1.call-start = ((), (), s32[]{:S(2)}) async-start(), calls=%async_computation.1 | async-start | bytes 2621440 | tf_op jit(solution)/shard_map/all_gather | solution.py:47
  8.3 8.3 %copy-start.6 = (f32[2,2,256,256]{3,2,1,0:T(8,128)S(1)}, f32[2,2,256,256]{3,2,1,0:T(8,128)}, u32[]{:S(2)}) copy-start(f32[2,2,256,256]{3,2,1,0:T(8,128)} %param.14) | copy-start | bytes 3145732
  8.3 3.6 collective-permute-start
  12.7 209.4 %all-reduce.4.cloned.1.call-start = ((), (), s32[]{:S(2)}) async-start(), calls=%async_computation.2 | async-start | bytes 4194304 | tf_op jit(solution)/shard_map/psum | solution.py:81
  137.6 1.0 copy-start.5
  137.6 2.0 copy-start.4
  137.7 84.5 %copy-start.7 = (bf16[8,256,256]{2,1,0:T(8,128)(2,1)S(1)}, bf16[8,256,256]{2,1,0:T(8,128)(2,1)}, u32[]{:S(2)}) copy-start(bf16[8,256,256]{2,1,0:T(8,128)(2,1)} %param.15) | copy-start | bytes 3145732
  137.7 432.0 %all-reduce.6.cloned.1.call-start = ((), (), s32[]{:S(2)}) async-start(), calls=%async_computation.4 | async-start | bytes 2621440 | tf_op jit(solution)/shard_map/psum | solution.py:128
  248.5 1.5 copy-start.2
  250.0 1.0 copy-start
  280.4 1.5 copy-start.2
  282.0 1.0 copy-start
  312.8 1.5 copy-start.2
  314.3 1.0 copy-start
  347.1 1.5 copy-start.2
  348.6 1.0 copy-start
  380.7 1.5 copy-start.2
  382.3 1.0 copy-start
  414.5 1.5 copy-start.2
  416.0 1.0 copy-start
  448.6 1.5 copy-start.2
  450.2 1.0 copy-start
  482.7 1.5 copy-start.2
  484.2 1.0 copy-start
  497.0 6.8 %copy-start.1 = (f32[2,2,256,256]{2,3,0,1:T(8,128)S(1)}, f32[2,2,256,256]{2,3,0,1:T(8,128)}, u32[]{:S(2)}) copy-start(f32[2,2,256,256]{2,3,0,1:T(8,128)} %get-tuple-element.159) | copy-start | bytes 3145732
  499.2 6.6 %collective-permute-start.1 = (bf16[3,256,1024]{2,1,0:T(8,128)(2,1)S(1)}, bf16[3,256,1024]{2,1,0:T(8,128)(2,1)}, u32[]{:S(2)}, u32[]{:S(2)}) collective-permute-start(bf16[3,256,1024]{2,1,0:T(8,128)(2,1)S(1)} %slice.165), channel_id=1, source_target_pairs={{0,4},{4,8},{8,12},{12,16},{16,20},{20,24},{24,28},{1,5},{5,9},{9,... | collective-permute-start | bytes 4718600 | tf_op jit(solution)/shard_map/ppermute | solution.py:14
  505.1 126.2 %reduce-scatter.2.cloned.1.call-start = ((), (), s32[]{:S(2)}) async-start(), calls=%async_computation.3 | async-start | bytes 3932160 | tf_op jit(solution)/shard_map/reduce_scatter | solution.py:125
  510.7 121.6 %copy-start.3 = (f32[2,256,256]{2,1,0:T(8,128)S(1)}, f32[2,256,256]{2,1,0:T(8,128)}, u32[]{:S(2)}) copy-start(f32[2,256,256]{2,1,0:T(8,128)} %param.13) | copy-start | bytes 1572868
Sparse Core Ops, SparseCore 0:
  12.8 52.6 all-gather.1
  137.8 84.3 all-reduce.3
  505.2 64.3 all-reduce.5
  571.8 59.5 reduce-scatter.1
where the time goes:
time: 647 us; the launch traced here: 641 us
  waiting for transfers between devices  247 us (38%)
  local copies, waits for them, and re-layouts  185 us (29%)
  other arithmetic  134 us (21%)
  loops' own time  31.6 us (5%)
  matrix products  22.2 us (3%)
  between operations  14.7 us (2%)
    psum x1, waiting for transfers between devices, shards(): intensity = lax.psum(local_power, 'tile')  79.3 us
    dynamic_update_slice x16, local copies, waits for them, and re-layouts, accumulate(): lax.dynamic_update_slice(buffer, region + numer, (zero_index, row_at, col...  72.4 us
    psum x1, waiting for transfers between devices, shards(): grad_total, weight_total = lax.psum((grad_sum, weight_sum), 'scan')  58.9 us
    reduce_scatter x1, waiting for transfers between devices, shards(): totals = lax.psum_scatter(own_rows, 'tile', scatter_dimension=2, tiled=True)  58.3 us
    all_gather x1, waiting for transfers between devices, shards(): band_all = lax.all_gather(extended, 'tile', axis=2, tiled=True)  47.6 us
    add x16, other arithmetic, accumulate(): return ((buffer, grad_sum + grads, weight_sum + live * weight), None)  35.4 us
    another operation x1, loops' own time, shards(): lax.scan(accumulate, init, (far_re, far_im, factor, windows, live_mask, r...  31.4 us
    gather x24, local copies, waits for them, and re-layouts  30.1 us
  transfers between devices with their start and end apart: 6, of which 6 were waited for; matrix products, arithmetic and copies ran while one was open for 3% of the time, Pallas kernels for 0%

commit v1 on v0

--- a/solution.py
+++ b/solution.py
@@ -78,7 +78,13 @@
         return (far_re, far_im, jnp.sum(far_re * far_re + far_im * far_im, axis=0))
 
     far_re, far_im, local_power = lax.map(forward_one, windows)
-    intensity = lax.psum(local_power, "tile")
+    size = lax.axis_size("tile")
+    intensity, stride = (local_power, 1)
+    while stride < size:
+        intensity = intensity + lax.ppermute(
+            intensity, "tile", [(i, i ^ stride) for i in range(size)]
+        )
+        stride = 2 * stride
     factor = live_mask[:, None, None] * (
         amplitudes.astype(jnp.float32) / jnp.maximum(jnp.sqrt(intensity), amp_floor) - 1.0
     )

time: 647 us -> 707 us (1.093)
  waiting for transfers between devices: 247 us -> 299 us
    ppermute x0 -> x2, waiting for transfers between devices: none -> 131 us  [shards(): lax.ppermute(intensity, 'tile', [(i, i ^ stride) for i in range(size)])]
    psum x1 -> x0, waiting for transfers between devices: 79.3 us -> none  [shards(): intensity = lax.psum(local_power, 'tile')]
  transfers between devices with their start and end apart: 6 -> 7, of which waited for: 6 -> 7; matrix products, arithmetic and copies ran while one was open for 3% -> 3% of each run, Pallas kernels for 0% -> 0%
where the time goes in v1:
time: 707 us; the launch traced here: 701 us
  waiting for transfers between devices  299 us (42%)
  local copies, waits for them, and re-layouts  185 us (26%)
  other arithmetic  136 us (19%)
  loops' own time  34.2 us (5%)
  matrix products  22.2 us (3%)
  between operations  14.6 us (2%)
  starting transfers between devices  9.85 us (1%)
    ppermute x2, waiting for transfers between devices, shards(): lax.ppermute(intensity, 'tile', [(i, i ^ stride) for i in range(size)])  131 us
    dynamic_update_slice x16, local copies, waits for them, and re-layouts, accumulate(): lax.dynamic_update_slice(buffer, region + numer, (zero_index, row_at, col...  72.5 us
    psum x1, waiting for transfers between devices, shards(): grad_total, weight_total = lax.psum((grad_sum, weight_sum), 'scan')  59.1 us
    reduce_scatter x1, waiting for transfers between devices, shards(): totals = lax.psum_scatter(own_rows, 'tile', scatter_dimension=2, tiled=True)  58.5 us
    all_gather x1, waiting for transfers between devices, shards(): band_all = lax.all_gather(extended, 'tile', axis=2, tiled=True)  47.6 us
    add x16, other arithmetic, accumulate(): return ((buffer, grad_sum + grads, weight_sum + live * weight), None)  35.8 us
    another operation x1, loops' own time, shards(): lax.scan(accumulate, init, (far_re, far_im, factor, windows, live_mask, r...  34 us
    gather x24, local copies, waits for them, and re-layouts  29.3 us
  transfers between devices with their start and end apart: 7, of which 7 were waited for; matrix products, arithmetic and copies ran while one was open for 3% of the time, Pallas kernels for 0%

profile of v1, /device:TPU:0, one launch (start us, length us, event | category | flops | bytes accessed | tf_op | source)
XLA Modules:
  0.0 701.3 jit_solution(12704562774946881168)
XLA Ops:
  18.0 47.6 %all-gather.2.cloned.1.call-done = bf16[2,512,1024]{2,1,0:T(8,128)(2,1)} async-done(((bf16[2,512,256]{2,1,0:T(8,128)(2,1)}), bf16[2,512,1024]{2,1,0:T(8,128)(2,1)}) %all-gather.2.cloned.1.call-update) | async-done | bytes 2097168 | tf_op jit(solution)/shard_map/all_gather | solution.py:47
  65.5 29.3 %while.33 = (s32[]{:T(128)}, bf16[2,512,1024]{2,1,0:T(8,128)(2,1)}, s32[8,3]{0,1:T(4,128)S(1)}, bf16[8,2,256,256]{3,2,1,0:T(8,128)(2,1)}, s32[]{:T(128)}) while((s32[]{:T(128)}, bf16[2,512,1024]{2,1,0:T(8,128)(2,1)}, s32[8,3]{0,1:T(4,128)S(1)}, bf16[8,2,256,256]{3,2,1,0:T(8,128)(2,1)}, s32[]{:T(128)}) %tuple.102), condition=%wide.while_cond.1, body=%wide.while_body.1.sunk | while | flops 2 | bytes 525429 | solution.py:53
  66.1 3.1 bitcast_dynamic-update-slice_fusion.6
  69.8 3.0 bitcast_dynamic-update-slice_fusion.6
  73.4 3.1 bitcast_dynamic-update-slice_fusion.6
  77.1 3.1 bitcast_dynamic-update-slice_fusion.6
  80.8 3.1 bitcast_dynamic-update-slice_fusion.6
  84.5 3.1 bitcast_dynamic-update-slice_fusion.6
  88.1 3.1 bitcast_dynamic-update-slice_fusion.6
  91.8 3.1 bitcast_dynamic-update-slice_fusion.6
  94.9 41.9 %while.32 = (s32[]{:T(128)}, f32[8,2,256,256]{2,3,1,0:T(8,128)}, f32[8,2,256,256]{2,3,1,0:T(8,128)}, f32[8,256,256]{2,1,0:T(8,128)}, bf16[8,2,256,256]{3,2,1,0:T...) while((s32[]{:T(128)}, f32[8,2,256,256]{2,3,1,0:T(8,128)}, ...), condition=%wide.region_2.3_spmd, body=%wide.region_0.2_spmd.sunk | while | flops 540344320 | bytes 12845209 | solution.py:80
  136.8 46.0 %collective-permute-done.1 = f32[8,256,256]{2,1,0:T(8,128)S(1)} collective-permute-done((f32[8,256,256]{2,1,0:T(8,128)}, f32[8,256,256]{2,1,0:T(8,128)S(1)}, u32[]{:S(2)}, u32[]{:S(2)}) %collective-permute-start.1) | collective-permute-done | bytes 2097184 | tf_op jit(solution)/shard_map/ppermute | solution.py:84
  184.8 3.3 collective-permute-start.2
  192.8 84.6 %collective-permute-done.2 = f32[8,256,256]{2,1,0:T(8,128)} collective-permute-done((f32[8,256,256]{2,1,0:T(8,128)S(1)}, f32[8,256,256]{2,1,0:T(8,128)}, u32[]{:S(2)}, u32[]{:S(2)}) %collective-permute-start.2) | collective-permute-done | bytes 2097184 | tf_op jit(solution)/shard_map/ppermute | solution.py:84
  277.5 4.1 add_multiply_fusion
  281.6 3.4 broadcast_in_dim.23.clone
  285.0 271.7 %while.34 = (s32[]{:T(128)}, f32[3,512,1024]{2,1,0:T(8,128)}, f32[2,2,256,256]{2,3,0,1:T(8,128)}, f32[256,256]{0,1:T(8,128)}, s32[8]{0:T(128)S(1)}, /*index=5*/s...) while((s32[]{:T(128)}, f32[3,512,1024]{2,1,0:T(8,128)}, ...), condition=%wide.region_7.8_spmd.clone, body=%wide.region_4.7_spmd.clone.sunk | while | flops 542769152 | bytes 35914140 | solution.py:124
  308.3 8.4 %dynamic_update_slice.23 = f32[3,512,1024]{2,1,0:T(8,128)} dynamic-update-slice(f32[3,512,1024]{2,1,0:T(8,128)} %get-tuple-element.660, f32[3,256,256]{2,1,0:T(8,128)S(1)} %copy.59, s32[]{:T(128)} %constant.100.clone.1..sunk.1, s32[]{:T(128)S(6)} %select_n.65, s32[]{:T(128)S(6)} %select_n.66) | dynamic-update-slice | bytes 1572868 | tf_op jit(solution)/shard_map/while/body/eval_jaxpr/dynamic_update_slice | solution.py:116
  324.0 2.4 select_add_fusion.2
  342.0 7.4 %dynamic_update_slice.23 = f32[3,512,1024]{2,1,0:T(8,128)} dynamic-update-slice(f32[3,512,1024]{2,1,0:T(8,128)} %get-tuple-element.660, f32[3,256,256]{2,1,0:T(8,128)S(1)} %copy.59, s32[]{:T(128)} %constant.100.clone.1..sunk.1, s32[]{:T(128)S(6)} %select_n.65, s32[]{:T(128)S(6)} %select_n.66) | dynamic-update-slice | bytes 1572868 | tf_op jit(solution)/shard_map/while/body/eval_jaxpr/dynamic_update_slice | solution.py:116
  374.8 9.4 %dynamic_update_slice.23 = f32[3,512,1024]{2,1,0:T(8,128)} dynamic-update-slice(f32[3,512,1024]{2,1,0:T(8,128)} %get-tuple-element.660, f32[3,256,256]{2,1,0:T(8,128)S(1)} %copy.59, s32[]{:T(128)} %constant.100.clone.1..sunk.1, s32[]{:T(128)S(6)} %select_n.65, s32[]{:T(128)S(6)} %select_n.66) | dynamic-update-slice | bytes 1572868 | tf_op jit(solution)/shard_map/while/body/eval_jaxpr/dynamic_update_slice | solution.py:116
  409.7 8.7 %dynamic_update_slice.23 = f32[3,512,1024]{2,1,0:T(8,128)} dynamic-update-slice(f32[3,512,1024]{2,1,0:T(8,128)} %get-tuple-element.660, f32[3,256,256]{2,1,0:T(8,128)S(1)} %copy.59, s32[]{:T(128)} %constant.100.clone.1..sunk.1, s32[]{:T(128)S(6)} %select_n.65, s32[]{:T(128)S(6)} %select_n.66) | dynamic-update-slice | bytes 1572868 | tf_op jit(solution)/shard_map/while/body/eval_jaxpr/dynamic_update_slice | solution.py:116
  425.7 2.4 select_add_fusion.2
  443.8 8.8 %dynamic_update_slice.23 = f32[3,512,1024]{2,1,0:T(8,128)} dynamic-update-slice(f32[3,512,1024]{2,1,0:T(8,128)} %get-tuple-element.660, f32[3,256,256]{2,1,0:T(8,128)S(1)} %copy.59, s32[]{:T(128)} %constant.100.clone.1..sunk.1, s32[]{:T(128)S(6)} %select_n.65, s32[]{:T(128)S(6)} %select_n.66) | dynamic-update-slice | bytes 1572868 | tf_op jit(solution)/shard_map/while/body/eval_jaxpr/dynamic_update_slice | solution.py:116
  478.1 9.3 %dynamic_update_slice.23 = f32[3,512,1024]{2,1,0:T(8,128)} dynamic-update-slice(f32[3,512,1024]{2,1,0:T(8,128)} %get-tuple-element.660, f32[3,256,256]{2,1,0:T(8,128)S(1)} %copy.59, s32[]{:T(128)} %constant.100.clone.1..sunk.1, s32[]{:T(128)S(6)} %select_n.65, s32[]{:T(128)S(6)} %select_n.66) | dynamic-update-slice | bytes 1572868 | tf_op jit(solution)/shard_map/while/body/eval_jaxpr/dynamic_update_slice | solution.py:116
  494.7 2.4 select_add_fusion.2
  512.8 9.2 %dynamic_update_slice.23 = f32[3,512,1024]{2,1,0:T(8,128)} dynamic-update-slice(f32[3,512,1024]{2,1,0:T(8,128)} %get-tuple-element.660, f32[3,256,256]{2,1,0:T(8,128)S(1)} %copy.59, s32[]{:T(128)} %constant.100.clone.1..sunk.1, s32[]{:T(128)S(6)} %select_n.65, s32[]{:T(128)S(6)} %select_n.66) | dynamic-update-slice | bytes 1572868 | tf_op jit(solution)/shard_map/while/body/eval_jaxpr/dynamic_update_slice | solution.py:116
  547.4 9.4 %dynamic_update_slice.23 = f32[3,512,1024]{2,1,0:T(8,128)} dynamic-update-slice(f32[3,512,1024]{2,1,0:T(8,128)} %get-tuple-element.660, f32[3,256,256]{2,1,0:T(8,128)S(1)} %copy.59, s32[]{:T(128)} %constant.100.clone.1..sunk.1, s32[]{:T(128)S(6)} %select_n.65, s32[]{:T(128)S(6)} %select_n.66) | dynamic-update-slice | bytes 1572868 | tf_op jit(solution)/shard_map/while/body/eval_jaxpr/dynamic_update_slice | solution.py:116
  559.0 5.0 collective-permute-start.3
  566.0 4.8 convert_add_fusion
  570.9 59.1 %all-reduce.3.cloned.1.call-done = (f32[2,2,256,256]{3,2,1,0:T(8,128)}, f32[256,256]{0,1:T(8,128)}) async-done(((f32[2,2,256,256]{3,2,1,0:T(8,128)}, f32[256,256]{0,1:T(8,128)}), (f32[2,2,256,256]{3,2,1,0:T(8,128)}, f32[256,256]{0,1:T(8,128)})) %all-reduce.3.cloned.1.call-update) | async-done | bytes 1310736 | tf_op jit(solution)/shard_map/psum | solution.py:134
  633.4 58.5 %reduce-scatter.2.cloned.1.call-done = f32[3,256,256]{2,1,0:T(8,128)} async-done(((f32[3,256,1024]{2,1,0:T(8,128)}), f32[3,256,256]{2,1,0:T(8,128)}) %reduce-scatter.2.cloned.1.call-update) | async-done | bytes 786448 | tf_op jit(solution)/shard_map/reduce_scatter | solution.py:131
  (327 shorter events, 233.7 us)
Async XLA Ops:
  7.2 5.7 copy-start.7
  7.2 58.4 %all-gather.2.cloned.1.call-start = ((), (), s32[]{:S(2)}) async-start(), calls=%async_computation.1 | async-start | bytes 2621440 | tf_op jit(solution)/shard_map/all_gather | solution.py:47
  8.3 8.3 %copy-start.6 = (f32[2,2,256,256]{3,2,1,0:T(8,128)S(1)}, f32[2,2,256,256]{3,2,1,0:T(8,128)}, u32[]{:S(2)}) copy-start(f32[2,2,256,256]{3,2,1,0:T(8,128)} %param.14) | copy-start | bytes 3145732
  8.3 3.6 collective-permute-start
  12.7 617.2 %all-reduce.3.cloned.1.call-start = ((), (), s32[]{:S(2)}) async-start(), calls=%async_computation.3 | async-start | bytes 2621440 | tf_op jit(solution)/shard_map/psum | solution.py:134
  136.7 52.0 %copy-start.5 = (f32[2,1,256,256]{3,2,1,0:T(8,128)S(1)}, f32[2,1,256,256]{3,2,1,0:T(8,128)}, u32[]{:S(2)}) copy-start(f32[2,1,256,256]{3,2,1,0:T(8,128)} %get-tuple-element.352) | copy-start | bytes 1572868
  136.7 53.0 %copy-start.4 = (f32[2,1,256,256]{3,2,1,0:T(8,128)S(1)}, f32[2,1,256,256]{3,2,1,0:T(8,128)}, u32[]{:S(2)}) copy-start(f32[2,1,256,256]{3,2,1,0:T(8,128)} %get-tuple-element.355) | copy-start | bytes 1572868
  136.8 46.0 %collective-permute-start.1 = (f32[8,256,256]{2,1,0:T(8,128)}, f32[8,256,256]{2,1,0:T(8,128)S(1)}, u32[]{:S(2)}, u32[]{:S(2)}) collective-permute-start(f32[8,256,256]{2,1,0:T(8,128)} %get-tuple-element.155), channel_id=1, source_target_pairs={{0,1},{1,0},{2,3},{3,2},{4,5},{5,4},{6,7},{7,6},{8,9},{9,8},{10,11... | collective-permute-start | bytes 6291464 | tf_op jit(solution)/shard_map/ppermute | solution.py:84
  184.8 92.6 %collective-permute-start.2 = (f32[8,256,256]{2,1,0:T(8,128)S(1)}, f32[8,256,256]{2,1,0:T(8,128)}, u32[]{:S(2)}, u32[]{:S(2)}) collective-permute-start(f32[8,256,256]{2,1,0:T(8,128)S(1)} %add.118), channel_id=1, source_target_pairs={{0,2},{1,3},{2,0},{3,1},{4,6},{5,7},{6,4},{7,5},{8,10},{9,11},{10,... | collective-permute-start | bytes 6291464 | tf_op jit(solution)/shard_map/ppermute | solution.py:84
  304.7 1.5 copy-start.2
  306.2 1.0 copy-start
  337.1 1.5 copy-start.2
  338.6 1.0 copy-start
  369.9 1.5 copy-start.2
  371.5 1.0 copy-start
  404.8 1.5 copy-start.2
  406.3 1.0 copy-start
  438.9 1.5 copy-start.2
  440.4 1.0 copy-start
  473.2 1.5 copy-start.2
  474.7 1.0 copy-start
  507.9 1.5 copy-start.2
  509.4 1.0 copy-start
  542.5 1.5 copy-start.2
  544.0 1.0 copy-start
  556.8 7.2 %copy-start.1 = (f32[2,2,256,256]{2,3,0,1:T(8,128)S(1)}, f32[2,2,256,256]{2,3,0,1:T(8,128)}, u32[]{:S(2)}) copy-start(f32[2,2,256,256]{2,3,0,1:T(8,128)} %get-tuple-element.159) | copy-start | bytes 3145732
  559.0 7.0 collective-permute-start.3
  565.3 126.5 %reduce-scatter.2.cloned.1.call-start = ((), (), s32[]{:S(2)}) async-start(), calls=%async_computation.2 | async-start | bytes 3932160 | tf_op jit(solution)/shard_map/reduce_scatter | solution.py:131
  570.9 121.9 %copy-start.3 = (f32[2,256,256]{2,1,0:T(8,128)S(1)}, f32[2,256,256]{2,1,0:T(8,128)}, u32[]{:S(2)}) copy-start(f32[2,256,256]{2,1,0:T(8,128)} %param.13) | copy-start | bytes 1572868
Sparse Core Ops, SparseCore 0:
  12.8 52.6 all-gather.1
  565.4 64.4 all-reduce.2
  632.3 59.5 reduce-scatter.1
